TPU v7x, 512 devices: a whole 4x4x16 slice. The times are simulated.
512 devices in a mesh: dom: 128 (over x, z, core), blk: 4 (over y).
Axes of the slice: x: 4, y: 4, z: 16, core: 2. Of those that a mesh axis runs over, the one named last changes fastest.
Arguments:
- degree: int32 [1024], P('dom'), may hold values from 1 to 3
- face_elem: int32 [4096], P('dom'), may hold values from 0 to 7
- face_side: int32 [4096], P('dom'), may hold values from 0 to 8, as said below
- face_peer: int32 [4096], P('dom'), may hold values from 0 to 7
- coupling: bfloat16 [4096, 320, 320], P('dom', 'blk'), may hold values from -0.078125 to 0.078125
- inv_diag: float32 [1024, 320], P('dom', 'blk'), may hold values from 0.5 to 2
- inv_off: bfloat16 [1024, 320, 320], P('dom', 'blk'), may hold values from -0.109375 to 0.109375
- source: float32 [1024, 320], P('dom', 'blk'), may hold values from -6 to 6
- residual: float32 [1024, 320], P('dom', 'blk'), may hold values from -0.6 to 0.6
Outputs:
- adjoint: float32 [1024, 320], P('dom', 'blk')
- indicator: float32 [1024], P('dom')
Inputs may be any that keep to these rules, and one draw needn't show every extreme that they name: `face_side`: among the 32 faces of one partition (aligned blocks of 32 rows) each side from 1 to 8 is named by at least 2 and at most 4 faces, and one side by exactly 4; the remaining faces have side 0.
All inputs are finite; a program needn't handle non-finite values.
Results may differ from a plain program's by a relative error of at most 0.004.
Values may be sent and summed in bfloat16 or wider, within the bound.
No kernel may reach another device: no remote copies, remote signals or barrier semaphores. Data moves between devices by JAX's collectives and lax.ppermute only.
A program may use at most 64 MiB of HBM per device.

v0:
```python
import jax
import jax.numpy as jnp
from jax import lax
from jax.sharding import PartitionSpec as P

MODES = 64
SWEEPS = 2
NEIGH = 8


def from_behind(block, axis, distance):
    devices = range(lax.axis_size(axis))
    route = [((i - distance) % len(devices), i) for i in devices]
    return lax.ppermute(block, axis, route)


def full_rows(values):
    return lax.all_gather(values, "blk", axis=1, tiled=True)


def local(degree, face_elem, face_side, face_peer, coupling, inv_diag, inv_off, source, residual):
    width = coupling.shape[2]
    quarter = source.shape[1]
    elements = source.shape[0]
    faces = coupling.shape[0]
    neigh = NEIGH
    half_count = neigh // 2
    capacity = faces // neigh
    offsets = [step_size for step_size in range(1, half_count + 1)] + [
        -step_size for step_size in range(1, half_count + 1)
    ]
    first_row = lax.axis_index("blk") * quarter
    limit = (degree + 1) ** 3 * MODES // 64
    modes = jnp.arange(width, dtype=jnp.int32) % MODES
    mask_full = (modes[None, :] < limit[:, None]).astype(jnp.float32)
    mask_rows = lax.dynamic_slice_in_dim(mask_full, first_row, quarter, 1)
    codes = jnp.arange(neigh + 1, dtype=jnp.int32)
    onehot = (face_side[:, None] == codes[None, :]).astype(jnp.int32)
    before = jnp.cumsum(onehot, axis=0) - onehot
    slot_index = jnp.sum(before * onehot, axis=1)
    crossing = face_side > 0
    inner = jnp.where(crossing, 0.0, 1.0).astype(jnp.float32)
    position = jnp.where(crossing, (face_side - 1) * capacity + slot_index, neigh * capacity)
    safe_position = jnp.minimum(position, neigh * capacity - 1)
    wanted = (
        jnp.zeros((neigh * capacity,), jnp.int32)
        .at[position]
        .set(face_peer, mode="drop")
        .reshape(neigh, capacity)
    )
    requested = jnp.stack(
        [from_behind(wanted[side_num], "dom", offsets[side_num]) for side_num in range(neigh)]
    )
    requested_flat = requested.reshape(-1)

    def invert(values_full):
        own_part = lax.dynamic_slice_in_dim(values_full, first_row, quarter, 1)
        product = jnp.einsum("eij,ej->ei", inv_off, values_full, preferred_element_type=jnp.float32)
        return inv_diag * own_part.astype(jnp.float32) + product

    source_half = (source * mask_rows).astype(jnp.bfloat16)
    base_state = invert(full_rows(source_half)) * mask_rows
    adjoint = base_state
    for sweep_index in range(SWEEPS):
        state_rows = adjoint.astype(jnp.bfloat16)
        state_full = full_rows(state_rows)
        outgoing = state_full[requested]
        incoming = jnp.stack(
            [
                from_behind(outgoing[side_num], "dom", -offsets[side_num])
                for side_num in range(neigh)
            ]
        ).reshape(-1, width)
        peer_state = jnp.where(crossing[:, None], incoming[safe_position], state_full[face_peer])
        elem_state = state_rows[face_elem]
        local_terms = jnp.einsum(
            "fij,fj->fi", coupling, peer_state, preferred_element_type=jnp.float32
        )
        transposed = jnp.einsum(
            "fij,fi->fj", coupling, elem_state, preferred_element_type=jnp.float32
        )
        own_terms = jnp.zeros((elements, quarter), jnp.float32).at[face_elem].add(local_terms)
        partial_value = (
            jnp.zeros((elements, width), jnp.float32).at[face_peer].add(transposed * inner[:, None])
        )
        outbound = (
            jnp.zeros((neigh * capacity, width), jnp.float32)
            .at[position]
            .set(transposed, mode="drop")
            .reshape(neigh, capacity, width)
        )
        returned = jnp.stack(
            [from_behind(outbound[side_num], "dom", offsets[side_num]) for side_num in range(neigh)]
        ).reshape(-1, width)
        partial_value = partial_value.at[requested_flat].add(returned)
        middle = lax.dynamic_slice_in_dim(partial_value, first_row, quarter, 1) + own_terms
        partial_value = lax.dynamic_update_slice_in_dim(partial_value, middle, first_row, 1)
        summed = lax.psum(partial_value, "blk")
        coupled_half = (summed * mask_full).astype(jnp.bfloat16)
        adjoint = (base_state - invert(coupled_half)) * mask_rows
    weights = jnp.sum(adjoint * residual * mask_rows, axis=1)
    indicator = lax.psum(weights, "blk")
    return (adjoint, indicator)


def solution(mesh):
    in_specs = (
        P("dom"),
        P("dom"),
        P("dom"),
        P("dom"),
        P("dom", "blk", None),
        P("dom", "blk"),
        P("dom", "blk", None),
        P("dom", "blk"),
        P("dom", "blk"),
    )
    out_specs = (P("dom", "blk"), P("dom"))
    return jax.shard_map(local, mesh=mesh, in_specs=in_specs, out_specs=out_specs, check_vma=False)
```

profile of v0, /device:TPU:64, one launch (start us, length us, event | category | flops | bytes accessed | tf_op | source)
XLA Modules:
  0.0 313.2 jit_solution(9358824529545259234)
XLA Ops:
  5.9 3.8 %collective-permute-start.1 = (s32[4]{0:T(128)S(1)}, s32[4]{0:T(128)S(1)}, u32[]{:S(2)}, u32[]{:S(2)}) collective-permute-start(s32[4]{0:T(128)S(1)} %get-tuple-element.44), channel_id=1, source_target_pairs={{504,0},{508,4},{0,8},{4,12},{8,16},{12,20},{16,24},{20,28},{24,32... | collective-permute-start | bytes 56 | tf_op jit(solution)/shard_map/ppermute | solution.py:14
  9.7 6.4 %collective-permute-start.2 = (s32[4]{0:T(128)S(1)}, s32[4]{0:T(128)S(1)}, u32[]{:S(2)}, u32[]{:S(2)}) collective-permute-start(s32[4]{0:T(128)S(1)} %get-tuple-element.43), channel_id=1, source_target_pairs={{500,0},{504,4},{508,8},{0,12},{4,16},{8,20},{12,24},{16,28},{20,3... | collective-permute-start | bytes 56 | tf_op jit(solution)/shard_map/ppermute | solution.py:14
  16.1 5.2 %collective-permute-start.3 = (s32[4]{0:T(128)S(1)}, s32[4]{0:T(128)S(1)}, u32[]{:S(2)}, u32[]{:S(2)}) collective-permute-start(s32[4]{0:T(128)S(1)} %get-tuple-element.42), channel_id=1, source_target_pairs={{496,0},{500,4},{504,8},{508,12},{0,16},{4,20},{8,24},{12,28},{16,... | collective-permute-start | bytes 56 | tf_op jit(solution)/shard_map/ppermute | solution.py:14
  21.3 1.9 collective-permute-start.4
  26.7 11.3 %all-gather = bf16[4,80,8]{1,2,0:T(8,128)(2,1)S(1)} all-gather(bf16[1,80,8]{1,2,0:T(8,128)(2,1)S(1)} %fusion.36), channel_id=1, replica_groups=mesh['dom'=128,'blk'=4] {'blk'}, dimensions={0}, use_global_device_ids=true | all-gather | bytes 6400 | tf_op jit(solution)/shard_map/all_gather | solution.py:18
  43.5 10.4 %all-gather.1 = bf16[4,80,8]{1,2,0:T(8,128)(2,1)S(1)} all-gather(bf16[1,80,8]{1,2,0:T(8,128)(2,1)S(1)} %bitcast.165), channel_id=1, replica_groups=mesh['dom'=128,'blk'=4] {'blk'}, dimensions={0}, use_global_device_ids=true | all-gather | bytes 6400 | tf_op jit(solution)/shard_map/all_gather | solution.py:18
  54.7 2.0 collective-permute-start.5
  56.7 1.9 collective-permute-start.6
  58.7 5.2 %collective-permute-start.7 = (s32[4]{0:T(128)S(1)}, s32[4]{0:T(128)S(1)}, u32[]{:S(2)}, u32[]{:S(2)}) collective-permute-start(s32[4]{0:T(128)S(1)} %get-tuple-element.38), channel_id=1, source_target_pairs={{16,0},{20,4},{24,8},{28,12},{32,16},{36,20},{40,24},{44,28},{48,3... | collective-permute-start | bytes 56 | tf_op jit(solution)/shard_map/ppermute | solution.py:14
  63.9 3.5 %collective-permute-start.8 = (f32[4,320]{1,0:T(4,128)S(1)}, f32[4,320]{1,0:T(4,128)S(1)}, u32[]{:S(2)}, u32[]{:S(2)}) collective-permute-start(f32[4,320]{1,0:T(4,128)S(1)} %get-tuple-element.21), channel_id=1, source_target_pairs={{508,0},{0,4},{4,8},{8,12},{12,16},{16,20},{20,24},{24,28},{28,32}... | collective-permute-start | bytes 15368 | tf_op jit(solution)/shard_map/ppermute | solution.py:14
  67.4 2.2 collective-permute-start.9
  69.6 3.9 %collective-permute-start.10 = (f32[4,320]{1,0:T(4,128)S(1)}, f32[4,320]{1,0:T(4,128)S(1)}, u32[]{:S(2)}, u32[]{:S(2)}) collective-permute-start(f32[4,320]{1,0:T(4,128)S(1)} %get-tuple-element.19), channel_id=1, source_target_pairs={{500,0},{504,4},{508,8},{0,12},{4,16},{8,20},{12,24},{16,28},{20,3... | collective-permute-start | bytes 15368 | tf_op jit(solution)/shard_map/ppermute | solution.py:14
  73.6 4.8 %collective-permute-start.11 = (f32[4,320]{1,0:T(4,128)S(1)}, f32[4,320]{1,0:T(4,128)S(1)}, u32[]{:S(2)}, u32[]{:S(2)}) collective-permute-start(f32[4,320]{1,0:T(4,128)S(1)} %get-tuple-element.18), channel_id=1, source_target_pairs={{496,0},{500,4},{504,8},{508,12},{0,16},{4,20},{8,24},{12,28},{16,... | collective-permute-start | bytes 15368 | tf_op jit(solution)/shard_map/ppermute | solution.py:14
  79.4 2.2 collective-permute-start.16
  82.8 2.5 collective-permute-start.17
  85.3 3.1 collective-permute-done.17
  88.4 8.1 %collective-permute-start.18 = (bf16[4,320]{1,0:T(4,128)(2,1)S(1)}, bf16[4,320]{1,0:T(4,128)(2,1)S(1)}, u32[]{:S(2)}, u32[]{:S(2)}) collective-permute-start(bf16[4,320]{1,0:T(4,128)(2,1)S(1)} %get-tuple-element.35), channel_id=1, source_target_pairs={{12,0},{16,4},{20,8},{24,12},{28,16},{32,20},{36,24},{40,28},{44,3... | collective-permute-start | bytes 7688 | tf_op jit(solution)/shard_map/ppermute | solution.py:14
  97.8 3.6 %collective-permute-start.19 = (bf16[4,320]{1,0:T(4,128)(2,1)S(1)}, bf16[4,320]{1,0:T(4,128)(2,1)S(1)}, u32[]{:S(2)}, u32[]{:S(2)}) collective-permute-start(bf16[4,320]{1,0:T(4,128)(2,1)S(1)} %get-tuple-element.34), channel_id=1, source_target_pairs={{16,0},{20,4},{24,8},{28,12},{32,16},{36,20},{40,24},{44,28},{48,3... | collective-permute-start | bytes 7688 | tf_op jit(solution)/shard_map/ppermute | solution.py:14
  101.5 4.0 %collective-permute-done.19 = bf16[4,320]{1,0:T(4,128)(2,1)S(1)} collective-permute-done((bf16[4,320]{1,0:T(4,128)(2,1)S(1)}, bf16[4,320]{1,0:T(4,128)(2,1)S(1)}, u32[]{:S(2)}, u32[]{:S(2)}) %collective-permute-start.19) | collective-permute-done | bytes 2592 | tf_op jit(solution)/shard_map/ppermute | solution.py:14
  107.4 7.2 %collective-permute-done.20 = bf16[4,320]{1,0:T(4,128)(2,1)S(1)} collective-permute-done((bf16[4,320]{1,0:T(4,128)(2,1)S(1)}, bf16[4,320]{1,0:T(4,128)(2,1)S(1)}, u32[]{:S(2)}, u32[]{:S(2)}) %collective-permute-start.20) | collective-permute-done | bytes 2592 | tf_op jit(solution)/shard_map/ppermute | solution.py:14
  116.5 3.5 %collective-permute-done.21 = bf16[4,320]{1,0:T(4,128)(2,1)S(1)} collective-permute-done((bf16[4,320]{1,0:T(4,128)(2,1)S(1)}, bf16[4,320]{1,0:T(4,128)(2,1)S(1)}, u32[]{:S(2)}, u32[]{:S(2)}) %collective-permute-start.21) | collective-permute-done | bytes 2592 | tf_op jit(solution)/shard_map/ppermute | solution.py:14
  122.0 4.4 %collective-permute-done.22 = bf16[4,320]{1,0:T(4,128)(2,1)S(1)} collective-permute-done((bf16[4,320]{1,0:T(4,128)(2,1)S(1)}, bf16[4,320]{1,0:T(4,128)(2,1)S(1)}, u32[]{:S(2)}, u32[]{:S(2)}) %collective-permute-start.22) | collective-permute-done | bytes 2592 | tf_op jit(solution)/shard_map/ppermute | solution.py:14
  126.4 2.1 collective-permute-start.23
  128.6 13.6 %collective-permute-done.23 = bf16[4,320]{1,0:T(4,128)(2,1)S(1)} collective-permute-done((bf16[4,320]{1,0:T(4,128)(2,1)S(1)}, bf16[4,320]{1,0:T(4,128)(2,1)S(1)}, u32[]{:S(2)}, u32[]{:S(2)}) %collective-permute-start.23) | collective-permute-done | bytes 2592 | tf_op jit(solution)/shard_map/ppermute | solution.py:14
  145.6 3.4 %collective-permute-start.13 = (f32[4,320]{1,0:T(4,128)S(1)}, f32[4,320]{1,0:T(4,128)S(1)}, u32[]{:S(2)}, u32[]{:S(2)}) collective-permute-start(f32[4,320]{1,0:T(4,128)S(1)} %get-tuple-element.16), channel_id=1, source_target_pairs={{8,0},{12,4},{16,8},{20,12},{24,16},{28,20},{32,24},{36,28},{40,32... | collective-permute-start | bytes 15368 | tf_op jit(solution)/shard_map/ppermute | solution.py:14
  149.0 6.8 %collective-permute-start.14 = (f32[4,320]{1,0:T(4,128)S(1)}, f32[4,320]{1,0:T(4,128)S(1)}, u32[]{:S(2)}, u32[]{:S(2)}) collective-permute-start(f32[4,320]{1,0:T(4,128)S(1)} %get-tuple-element.15), channel_id=1, source_target_pairs={{12,0},{16,4},{20,8},{24,12},{28,16},{32,20},{36,24},{40,28},{44,3... | collective-permute-start | bytes 15368 | tf_op jit(solution)/shard_map/ppermute | solution.py:14
  155.9 1.9 collective-permute-start.15
  157.9 5.6 %collective-permute-done.15 = f32[4,320]{1,0:T(4,128)S(1)} collective-permute-done((f32[4,320]{1,0:T(4,128)S(1)}, f32[4,320]{1,0:T(4,128)S(1)}, u32[]{:S(2)}, u32[]{:S(2)}) %collective-permute-start.15) | collective-permute-done | bytes 5152 | tf_op jit(solution)/shard_map/ppermute | solution.py:14
  165.4 15.8 %psum.21 = bf16[8,320]{1,0:T(8,128)(2,1)S(1)} all-reduce(f32[8,320]{1,0:T(8,128)S(1)} %dynamic_update_slice.6), channel_id=1, replica_groups=mesh['dom'=128,'blk'=4] {'blk'}, use_global_device_ids=true, to_apply=%region_7.8 | all-reduce | flops 2560 | bytes 15360 | tf_op jit(solution)/shard_map/psum | solution.py:98
  183.4 10.4 %all-gather.2 = bf16[4,80,8]{1,2,0:T(8,128)(2,1)S(1)} all-gather(bf16[1,80,8]{1,2,0:T(8,128)(2,1)S(1)} %bitcast.166), channel_id=1, replica_groups=mesh['dom'=128,'blk'=4] {'blk'}, dimensions={0}, use_global_device_ids=true | all-gather | bytes 6400 | tf_op jit(solution)/shard_map/all_gather | solution.py:18
  198.0 2.4 collective-permute-start.24
  200.5 3.6 %collective-permute-start.25 = (f32[4,320]{1,0:T(4,128)S(1)}, f32[4,320]{1,0:T(4,128)S(1)}, u32[]{:S(2)}, u32[]{:S(2)}) collective-permute-start(f32[4,320]{1,0:T(4,128)S(1)} %get-tuple-element.12), channel_id=1, source_target_pairs={{504,0},{508,4},{0,8},{4,12},{8,16},{12,20},{16,24},{20,28},{24,32... | collective-permute-start | bytes 15368 | tf_op jit(solution)/shard_map/ppermute | solution.py:14
  204.1 1.9 collective-permute-start.26
  208.0 3.4 %collective-permute-start.33 = (bf16[4,320]{1,0:T(4,128)(2,1)S(1)}, bf16[4,320]{1,0:T(4,128)(2,1)S(1)}, u32[]{:S(2)}, u32[]{:S(2)}) collective-permute-start(bf16[4,320]{1,0:T(4,128)(2,1)S(1)} %get-tuple-element.28), channel_id=1, source_target_pairs={{8,0},{12,4},{16,8},{20,12},{24,16},{28,20},{32,24},{36,28},{40,32... | collective-permute-start | bytes 7688 | tf_op jit(solution)/shard_map/ppermute | solution.py:14
  211.4 2.1 collective-permute-done.33
  213.5 5.9 %collective-permute-start.34 = (bf16[4,320]{1,0:T(4,128)(2,1)S(1)}, bf16[4,320]{1,0:T(4,128)(2,1)S(1)}, u32[]{:S(2)}, u32[]{:S(2)}) collective-permute-start(bf16[4,320]{1,0:T(4,128)(2,1)S(1)} %get-tuple-element.27), channel_id=1, source_target_pairs={{12,0},{16,4},{20,8},{24,12},{28,16},{32,20},{36,24},{40,28},{44,3... | collective-permute-start | bytes 7688 | tf_op jit(solution)/shard_map/ppermute | solution.py:14
  220.7 5.3 %collective-permute-start.35 = (bf16[4,320]{1,0:T(4,128)(2,1)S(1)}, bf16[4,320]{1,0:T(4,128)(2,1)S(1)}, u32[]{:S(2)}, u32[]{:S(2)}) collective-permute-start(bf16[4,320]{1,0:T(4,128)(2,1)S(1)} %get-tuple-element.26), channel_id=1, source_target_pairs={{16,0},{20,4},{24,8},{28,12},{32,16},{36,20},{40,24},{44,28},{48,3... | collective-permute-start | bytes 7688 | tf_op jit(solution)/shard_map/ppermute | solution.py:14
  226.0 2.2 collective-permute-done.35
  228.3 3.1 collective-permute-start.36
  231.4 6.0 %collective-permute-done.36 = bf16[4,320]{1,0:T(4,128)(2,1)S(1)} collective-permute-done((bf16[4,320]{1,0:T(4,128)(2,1)S(1)}, bf16[4,320]{1,0:T(4,128)(2,1)S(1)}, u32[]{:S(2)}, u32[]{:S(2)}) %collective-permute-start.36) | collective-permute-done | bytes 2592 | tf_op jit(solution)/shard_map/ppermute | solution.py:14
  239.3 4.8 %collective-permute-done.37 = bf16[4,320]{1,0:T(4,128)(2,1)S(1)} collective-permute-done((bf16[4,320]{1,0:T(4,128)(2,1)S(1)}, bf16[4,320]{1,0:T(4,128)(2,1)S(1)}, u32[]{:S(2)}, u32[]{:S(2)}) %collective-permute-start.37) | collective-permute-done | bytes 2592 | tf_op jit(solution)/shard_map/ppermute | solution.py:14
  246.1 4.6 %collective-permute-done.38 = bf16[4,320]{1,0:T(4,128)(2,1)S(1)} collective-permute-done((bf16[4,320]{1,0:T(4,128)(2,1)S(1)}, bf16[4,320]{1,0:T(4,128)(2,1)S(1)}, u32[]{:S(2)}, u32[]{:S(2)}) %collective-permute-start.38) | collective-permute-done | bytes 2592 | tf_op jit(solution)/shard_map/ppermute | solution.py:14
  252.7 12.3 %collective-permute-done.39 = bf16[4,320]{1,0:T(4,128)(2,1)S(1)} collective-permute-done((bf16[4,320]{1,0:T(4,128)(2,1)S(1)}, bf16[4,320]{1,0:T(4,128)(2,1)S(1)}, u32[]{:S(2)}, u32[]{:S(2)}) %collective-permute-start.39) | collective-permute-done | bytes 2592 | tf_op jit(solution)/shard_map/ppermute | solution.py:14
  268.4 3.4 %collective-permute-start.29 = (f32[4,320]{1,0:T(4,128)S(1)}, f32[4,320]{1,0:T(4,128)S(1)}, u32[]{:S(2)}, u32[]{:S(2)}) collective-permute-start(f32[4,320]{1,0:T(4,128)S(1)} %get-tuple-element.8), channel_id=1, source_target_pairs={{8,0},{12,4},{16,8},{20,12},{24,16},{28,20},{32,24},{36,28},{40,32... | collective-permute-start | bytes 15368 | tf_op jit(solution)/shard_map/ppermute | solution.py:14
  271.9 6.8 %collective-permute-start.30 = (f32[4,320]{1,0:T(4,128)S(1)}, f32[4,320]{1,0:T(4,128)S(1)}, u32[]{:S(2)}, u32[]{:S(2)}) collective-permute-start(f32[4,320]{1,0:T(4,128)S(1)} %get-tuple-element.7), channel_id=1, source_target_pairs={{12,0},{16,4},{20,8},{24,12},{28,16},{32,20},{36,24},{40,28},{44,3... | collective-permute-start | bytes 15368 | tf_op jit(solution)/shard_map/ppermute | solution.py:14
  280.7 5.6 %collective-permute-done.31 = f32[4,320]{1,0:T(4,128)S(1)} collective-permute-done((f32[4,320]{1,0:T(4,128)S(1)}, f32[4,320]{1,0:T(4,128)S(1)}, u32[]{:S(2)}, u32[]{:S(2)}) %collective-permute-start.31) | collective-permute-done | bytes 5152 | tf_op jit(solution)/shard_map/ppermute | solution.py:14
  288.2 14.3 %psum.22 = bf16[8,320]{1,0:T(8,128)(2,1)S(1)} all-reduce(f32[8,320]{1,0:T(8,128)S(1)} %dynamic_update_slice.7), channel_id=1, replica_groups=mesh['dom'=128,'blk'=4] {'blk'}, use_global_device_ids=true, to_apply=%region_12.13 | all-reduce | flops 2560 | bytes 15360 | tf_op jit(solution)/shard_map/psum | solution.py:98
  303.7 9.5 %psum.23 = f32[8]{0:T(128)} all-reduce(f32[8]{0:T(128)S(1)} %get-tuple-element.2), channel_id=1, replica_groups=mesh['dom'=128,'blk'=4] {'blk'}, use_global_device_ids=true, to_apply=%region_14.15 | all-reduce | flops 8 | bytes 64 | tf_op jit(solution)/shard_map/psum | solution.py:102
  (160 shorter events, 53.5 us)
Async XLA Ops:
  0.6 40.9 %copy-start = (bf16[32,80,320]{2,1,0:T(8,128)(2,1)S(1)}, bf16[32,80,320]{2,1,0:T(8,128)(2,1)}, u32[]{:S(2)}) copy-start(bf16[32,80,320]{2,1,0:T(8,128)(2,1)} %param.13) | copy-start | bytes 4915204
  4.0 50.7 %collective-permute-start = (s32[4]{0:T(128)S(1)}, s32[4]{0:T(128)S(1)}, u32[]{:S(2)}, u32[]{:S(2)}) collective-permute-start(s32[4]{0:T(128)S(1)} %get-tuple-element.45), channel_id=1, source_target_pairs={{508,0},{0,4},{4,8},{8,12},{12,16},{16,20},{20,24},{24,28},{28,32}... | collective-permute-start | bytes 56 | tf_op jit(solution)/shard_map/ppermute | solution.py:14
  5.9 50.8 %collective-permute-start.1 = (s32[4]{0:T(128)S(1)}, s32[4]{0:T(128)S(1)}, u32[]{:S(2)}, u32[]{:S(2)}) collective-permute-start(s32[4]{0:T(128)S(1)} %get-tuple-element.44), channel_id=1, source_target_pairs={{504,0},{508,4},{0,8},{4,12},{8,16},{12,20},{16,24},{20,28},{24,32... | collective-permute-start | bytes 56 | tf_op jit(solution)/shard_map/ppermute | solution.py:14
  9.7 48.9 %collective-permute-start.2 = (s32[4]{0:T(128)S(1)}, s32[4]{0:T(128)S(1)}, u32[]{:S(2)}, u32[]{:S(2)}) collective-permute-start(s32[4]{0:T(128)S(1)} %get-tuple-element.43), channel_id=1, source_target_pairs={{500,0},{504,4},{508,8},{0,12},{4,16},{8,20},{12,24},{16,28},{20,3... | collective-permute-start | bytes 56 | tf_op jit(solution)/shard_map/ppermute | solution.py:14
  16.1 47.8 %collective-permute-start.3 = (s32[4]{0:T(128)S(1)}, s32[4]{0:T(128)S(1)}, u32[]{:S(2)}, u32[]{:S(2)}) collective-permute-start(s32[4]{0:T(128)S(1)} %get-tuple-element.42), channel_id=1, source_target_pairs={{496,0},{500,4},{504,8},{508,12},{0,16},{4,20},{8,24},{12,28},{16,... | collective-permute-start | bytes 56 | tf_op jit(solution)/shard_map/ppermute | solution.py:14
  21.3 46.1 %collective-permute-start.4 = (s32[4]{0:T(128)S(1)}, s32[4]{0:T(128)S(1)}, u32[]{:S(2)}, u32[]{:S(2)}) collective-permute-start(s32[4]{0:T(128)S(1)} %get-tuple-element.41), channel_id=1, source_target_pairs={{4,0},{8,4},{12,8},{16,12},{20,16},{24,20},{28,24},{32,28},{36,32}... | collective-permute-start | bytes 56 | tf_op jit(solution)/shard_map/ppermute | solution.py:14
  54.7 14.9 %collective-permute-start.5 = (s32[4]{0:T(128)S(1)}, s32[4]{0:T(128)S(1)}, u32[]{:S(2)}, u32[]{:S(2)}) collective-permute-start(s32[4]{0:T(128)S(1)} %get-tuple-element.40), channel_id=1, source_target_pairs={{8,0},{12,4},{16,8},{20,12},{24,16},{28,20},{32,24},{36,28},{40,32... | collective-permute-start | bytes 56 | tf_op jit(solution)/shard_map/ppermute | solution.py:14
  56.7 16.8 %collective-permute-start.6 = (s32[4]{0:T(128)S(1)}, s32[4]{0:T(128)S(1)}, u32[]{:S(2)}, u32[]{:S(2)}) collective-permute-start(s32[4]{0:T(128)S(1)} %get-tuple-element.39), channel_id=1, source_target_pairs={{12,0},{16,4},{20,8},{24,12},{28,16},{32,20},{36,24},{40,28},{44,3... | collective-permute-start | bytes 56 | tf_op jit(solution)/shard_map/ppermute | solution.py:14
  58.7 19.7 %collective-permute-start.7 = (s32[4]{0:T(128)S(1)}, s32[4]{0:T(128)S(1)}, u32[]{:S(2)}, u32[]{:S(2)}) collective-permute-start(s32[4]{0:T(128)S(1)} %get-tuple-element.38), channel_id=1, source_target_pairs={{16,0},{20,4},{24,8},{28,12},{32,16},{36,20},{40,24},{44,28},{48,3... | collective-permute-start | bytes 56 | tf_op jit(solution)/shard_map/ppermute | solution.py:14
  63.9 81.7 %collective-permute-start.8 = (f32[4,320]{1,0:T(4,128)S(1)}, f32[4,320]{1,0:T(4,128)S(1)}, u32[]{:S(2)}, u32[]{:S(2)}) collective-permute-start(f32[4,320]{1,0:T(4,128)S(1)} %get-tuple-element.21), channel_id=1, source_target_pairs={{508,0},{0,4},{4,8},{8,12},{12,16},{16,20},{20,24},{24,28},{28,32}... | collective-permute-start | bytes 15368 | tf_op jit(solution)/shard_map/ppermute | solution.py:14
  67.4 81.6 %collective-permute-start.9 = (f32[4,320]{1,0:T(4,128)S(1)}, f32[4,320]{1,0:T(4,128)S(1)}, u32[]{:S(2)}, u32[]{:S(2)}) collective-permute-start(f32[4,320]{1,0:T(4,128)S(1)} %get-tuple-element.20), channel_id=1, source_target_pairs={{504,0},{508,4},{0,8},{4,12},{8,16},{12,20},{16,24},{20,28},{24,32... | collective-permute-start | bytes 15368 | tf_op jit(solution)/shard_map/ppermute | solution.py:14
  69.6 86.2 %collective-permute-start.10 = (f32[4,320]{1,0:T(4,128)S(1)}, f32[4,320]{1,0:T(4,128)S(1)}, u32[]{:S(2)}, u32[]{:S(2)}) collective-permute-start(f32[4,320]{1,0:T(4,128)S(1)} %get-tuple-element.19), channel_id=1, source_target_pairs={{500,0},{504,4},{508,8},{0,12},{4,16},{8,20},{12,24},{16,28},{20,3... | collective-permute-start | bytes 15368 | tf_op jit(solution)/shard_map/ppermute | solution.py:14
  73.6 84.2 %collective-permute-start.11 = (f32[4,320]{1,0:T(4,128)S(1)}, f32[4,320]{1,0:T(4,128)S(1)}, u32[]{:S(2)}, u32[]{:S(2)}) collective-permute-start(f32[4,320]{1,0:T(4,128)S(1)} %get-tuple-element.18), channel_id=1, source_target_pairs={{496,0},{500,4},{504,8},{508,12},{0,16},{4,20},{8,24},{12,28},{16,... | collective-permute-start | bytes 15368 | tf_op jit(solution)/shard_map/ppermute | solution.py:14
  79.3 102.0 %copy-start.3 = (bf16[8,80,320]{2,1,0:T(8,128)(2,1)S(1)}, bf16[8,80,320]{2,1,0:T(8,128)(2,1)}, u32[]{:S(2)}) copy-start(bf16[8,80,320]{2,1,0:T(8,128)(2,1)} %param.15) | copy-start | bytes 1228804
  79.4 3.5 %collective-permute-start.16 = (bf16[4,320]{1,0:T(4,128)(2,1)S(1)}, bf16[4,320]{1,0:T(4,128)(2,1)S(1)}, u32[]{:S(2)}, u32[]{:S(2)}) collective-permute-start(bf16[4,320]{1,0:T(4,128)(2,1)S(1)} %get-tuple-element.37), channel_id=1, source_target_pairs={{4,0},{8,4},{12,8},{16,12},{20,16},{24,20},{28,24},{32,28},{36,32}... | collective-permute-start | bytes 7688 | tf_op jit(solution)/shard_map/ppermute | solution.py:14
  82.8 5.6 %collective-permute-start.17 = (bf16[4,320]{1,0:T(4,128)(2,1)S(1)}, bf16[4,320]{1,0:T(4,128)(2,1)S(1)}, u32[]{:S(2)}, u32[]{:S(2)}) collective-permute-start(bf16[4,320]{1,0:T(4,128)(2,1)S(1)} %get-tuple-element.36), channel_id=1, source_target_pairs={{8,0},{12,4},{16,8},{20,12},{24,16},{28,20},{32,24},{36,28},{40,32... | collective-permute-start | bytes 7688 | tf_op jit(solution)/shard_map/ppermute | solution.py:14
  88.4 9.4 %collective-permute-start.18 = (bf16[4,320]{1,0:T(4,128)(2,1)S(1)}, bf16[4,320]{1,0:T(4,128)(2,1)S(1)}, u32[]{:S(2)}, u32[]{:S(2)}) collective-permute-start(bf16[4,320]{1,0:T(4,128)(2,1)S(1)} %get-tuple-element.35), channel_id=1, source_target_pairs={{12,0},{16,4},{20,8},{24,12},{28,16},{32,20},{36,24},{40,28},{44,3... | collective-permute-start | bytes 7688 | tf_op jit(solution)/shard_map/ppermute | solution.py:14
  97.8 7.6 %collective-permute-start.19 = (bf16[4,320]{1,0:T(4,128)(2,1)S(1)}, bf16[4,320]{1,0:T(4,128)(2,1)S(1)}, u32[]{:S(2)}, u32[]{:S(2)}) collective-permute-start(bf16[4,320]{1,0:T(4,128)(2,1)S(1)} %get-tuple-element.34), channel_id=1, source_target_pairs={{16,0},{20,4},{24,8},{28,12},{32,16},{36,20},{40,24},{44,28},{48,3... | collective-permute-start | bytes 7688 | tf_op jit(solution)/shard_map/ppermute | solution.py:14
  105.4 9.2 %collective-permute-start.20 = (bf16[4,320]{1,0:T(4,128)(2,1)S(1)}, bf16[4,320]{1,0:T(4,128)(2,1)S(1)}, u32[]{:S(2)}, u32[]{:S(2)}) collective-permute-start(bf16[4,320]{1,0:T(4,128)(2,1)S(1)} %get-tuple-element.33), channel_id=1, source_target_pairs={{508,0},{0,4},{4,8},{8,12},{12,16},{16,20},{20,24},{24,28},{28,32}... | collective-permute-start | bytes 7688 | tf_op jit(solution)/shard_map/ppermute | solution.py:14
  114.6 5.5 %collective-permute-start.21 = (bf16[4,320]{1,0:T(4,128)(2,1)S(1)}, bf16[4,320]{1,0:T(4,128)(2,1)S(1)}, u32[]{:S(2)}, u32[]{:S(2)}) collective-permute-start(bf16[4,320]{1,0:T(4,128)(2,1)S(1)} %get-tuple-element.32), channel_id=1, source_target_pairs={{504,0},{508,4},{0,8},{4,12},{8,16},{12,20},{16,24},{20,28},{24,32... | collective-permute-start | bytes 7688 | tf_op jit(solution)/shard_map/ppermute | solution.py:14
  120.1 6.4 %collective-permute-start.22 = (bf16[4,320]{1,0:T(4,128)(2,1)S(1)}, bf16[4,320]{1,0:T(4,128)(2,1)S(1)}, u32[]{:S(2)}, u32[]{:S(2)}) collective-permute-start(bf16[4,320]{1,0:T(4,128)(2,1)S(1)} %get-tuple-element.31), channel_id=1, source_target_pairs={{500,0},{504,4},{508,8},{0,12},{4,16},{8,20},{12,24},{16,28},{20,3... | collective-permute-start | bytes 7688 | tf_op jit(solution)/shard_map/ppermute | solution.py:14
  126.4 15.7 %collective-permute-start.23 = (bf16[4,320]{1,0:T(4,128)(2,1)S(1)}, bf16[4,320]{1,0:T(4,128)(2,1)S(1)}, u32[]{:S(2)}, u32[]{:S(2)}) collective-permute-start(bf16[4,320]{1,0:T(4,128)(2,1)S(1)} %get-tuple-element.30), channel_id=1, source_target_pairs={{496,0},{500,4},{504,8},{508,12},{0,16},{4,20},{8,24},{12,28},{16,... | collective-permute-start | bytes 7688 | tf_op jit(solution)/shard_map/ppermute | solution.py:14
  142.2 15.6 %collective-permute-start.12 = (f32[4,320]{1,0:T(4,128)S(1)}, f32[4,320]{1,0:T(4,128)S(1)}, u32[]{:S(2)}, u32[]{:S(2)}) collective-permute-start(f32[4,320]{1,0:T(4,128)S(1)} %get-tuple-element.17), channel_id=1, source_target_pairs={{4,0},{8,4},{12,8},{16,12},{20,16},{24,20},{28,24},{32,28},{36,32}... | collective-permute-start | bytes 15368 | tf_op jit(solution)/shard_map/ppermute | solution.py:14
  144.8 36.7 %copy-start.1 = (f32[8,80]{1,0:T(8,128)S(1)}, f32[8,80]{1,0:T(8,128)}, u32[]{:S(2)}) copy-start(f32[8,80]{1,0:T(8,128)} %param.14) | copy-start | bytes 7684
  145.6 12.2 %collective-permute-start.13 = (f32[4,320]{1,0:T(4,128)S(1)}, f32[4,320]{1,0:T(4,128)S(1)}, u32[]{:S(2)}, u32[]{:S(2)}) collective-permute-start(f32[4,320]{1,0:T(4,128)S(1)} %get-tuple-element.16), channel_id=1, source_target_pairs={{8,0},{12,4},{16,8},{20,12},{24,16},{28,20},{32,24},{36,28},{40,32... | collective-permute-start | bytes 15368 | tf_op jit(solution)/shard_map/ppermute | solution.py:14
  149.0 8.8 %collective-permute-start.14 = (f32[4,320]{1,0:T(4,128)S(1)}, f32[4,320]{1,0:T(4,128)S(1)}, u32[]{:S(2)}, u32[]{:S(2)}) collective-permute-start(f32[4,320]{1,0:T(4,128)S(1)} %get-tuple-element.15), channel_id=1, source_target_pairs={{12,0},{16,4},{20,8},{24,12},{28,16},{32,20},{36,24},{40,28},{44,3... | collective-permute-start | bytes 15368 | tf_op jit(solution)/shard_map/ppermute | solution.py:14
  155.9 7.6 %collective-permute-start.15 = (f32[4,320]{1,0:T(4,128)S(1)}, f32[4,320]{1,0:T(4,128)S(1)}, u32[]{:S(2)}, u32[]{:S(2)}) collective-permute-start(f32[4,320]{1,0:T(4,128)S(1)} %get-tuple-element.14), channel_id=1, source_target_pairs={{16,0},{20,4},{24,8},{28,12},{32,16},{36,20},{40,24},{44,28},{48,3... | collective-permute-start | bytes 15368 | tf_op jit(solution)/shard_map/ppermute | solution.py:14
  194.6 13.3 %collective-permute-start.32 = (bf16[4,320]{1,0:T(4,128)(2,1)S(1)}, bf16[4,320]{1,0:T(4,128)(2,1)S(1)}, u32[]{:S(2)}, u32[]{:S(2)}) collective-permute-start(bf16[4,320]{1,0:T(4,128)(2,1)S(1)} %get-tuple-element.29), channel_id=1, source_target_pairs={{4,0},{8,4},{12,8},{16,12},{20,16},{24,20},{28,24},{32,28},{36,32}... | collective-permute-start | bytes 7688 | tf_op jit(solution)/shard_map/ppermute | solution.py:14
  198.0 70.4 %collective-permute-start.24 = (f32[4,320]{1,0:T(4,128)S(1)}, f32[4,320]{1,0:T(4,128)S(1)}, u32[]{:S(2)}, u32[]{:S(2)}) collective-permute-start(f32[4,320]{1,0:T(4,128)S(1)} %get-tuple-element.13), channel_id=1, source_target_pairs={{508,0},{0,4},{4,8},{8,12},{12,16},{16,20},{20,24},{24,28},{28,32}... | collective-permute-start | bytes 15368 | tf_op jit(solution)/shard_map/ppermute | solution.py:14
  200.5 71.4 %collective-permute-start.25 = (f32[4,320]{1,0:T(4,128)S(1)}, f32[4,320]{1,0:T(4,128)S(1)}, u32[]{:S(2)}, u32[]{:S(2)}) collective-permute-start(f32[4,320]{1,0:T(4,128)S(1)} %get-tuple-element.12), channel_id=1, source_target_pairs={{504,0},{508,4},{0,8},{4,12},{8,16},{12,20},{16,24},{20,28},{24,32... | collective-permute-start | bytes 15368 | tf_op jit(solution)/shard_map/ppermute | solution.py:14
  204.1 74.6 %collective-permute-start.26 = (f32[4,320]{1,0:T(4,128)S(1)}, f32[4,320]{1,0:T(4,128)S(1)}, u32[]{:S(2)}, u32[]{:S(2)}) collective-permute-start(f32[4,320]{1,0:T(4,128)S(1)} %get-tuple-element.11), channel_id=1, source_target_pairs={{500,0},{504,4},{508,8},{0,12},{4,16},{8,20},{12,24},{16,28},{20,3... | collective-permute-start | bytes 15368 | tf_op jit(solution)/shard_map/ppermute | solution.py:14
  206.0 74.6 %collective-permute-start.27 = (f32[4,320]{1,0:T(4,128)S(1)}, f32[4,320]{1,0:T(4,128)S(1)}, u32[]{:S(2)}, u32[]{:S(2)}) collective-permute-start(f32[4,320]{1,0:T(4,128)S(1)} %get-tuple-element.10), channel_id=1, source_target_pairs={{496,0},{500,4},{504,8},{508,12},{0,16},{4,20},{8,24},{12,28},{16,... | collective-permute-start | bytes 15368 | tf_op jit(solution)/shard_map/ppermute | solution.py:14
  208.0 5.5 %collective-permute-start.33 = (bf16[4,320]{1,0:T(4,128)(2,1)S(1)}, bf16[4,320]{1,0:T(4,128)(2,1)S(1)}, u32[]{:S(2)}, u32[]{:S(2)}) collective-permute-start(bf16[4,320]{1,0:T(4,128)(2,1)S(1)} %get-tuple-element.28), channel_id=1, source_target_pairs={{8,0},{12,4},{16,8},{20,12},{24,16},{28,20},{32,24},{36,28},{40,32... | collective-permute-start | bytes 7688 | tf_op jit(solution)/shard_map/ppermute | solution.py:14
  213.5 7.2 %collective-permute-start.34 = (bf16[4,320]{1,0:T(4,128)(2,1)S(1)}, bf16[4,320]{1,0:T(4,128)(2,1)S(1)}, u32[]{:S(2)}, u32[]{:S(2)}) collective-permute-start(bf16[4,320]{1,0:T(4,128)(2,1)S(1)} %get-tuple-element.27), channel_id=1, source_target_pairs={{12,0},{16,4},{20,8},{24,12},{28,16},{32,20},{36,24},{40,28},{44,3... | collective-permute-start | bytes 7688 | tf_op jit(solution)/shard_map/ppermute | solution.py:14
  220.7 7.6 %collective-permute-start.35 = (bf16[4,320]{1,0:T(4,128)(2,1)S(1)}, bf16[4,320]{1,0:T(4,128)(2,1)S(1)}, u32[]{:S(2)}, u32[]{:S(2)}) collective-permute-start(bf16[4,320]{1,0:T(4,128)(2,1)S(1)} %get-tuple-element.26), channel_id=1, source_target_pairs={{16,0},{20,4},{24,8},{28,12},{32,16},{36,20},{40,24},{44,28},{48,3... | collective-permute-start | bytes 7688 | tf_op jit(solution)/shard_map/ppermute | solution.py:14
  228.3 9.2 %collective-permute-start.36 = (bf16[4,320]{1,0:T(4,128)(2,1)S(1)}, bf16[4,320]{1,0:T(4,128)(2,1)S(1)}, u32[]{:S(2)}, u32[]{:S(2)}) collective-permute-start(bf16[4,320]{1,0:T(4,128)(2,1)S(1)} %get-tuple-element.25), channel_id=1, source_target_pairs={{508,0},{0,4},{4,8},{8,12},{12,16},{16,20},{20,24},{24,28},{28,32}... | collective-permute-start | bytes 7688 | tf_op jit(solution)/shard_map/ppermute | solution.py:14
  237.4 6.8 %collective-permute-start.37 = (bf16[4,320]{1,0:T(4,128)(2,1)S(1)}, bf16[4,320]{1,0:T(4,128)(2,1)S(1)}, u32[]{:S(2)}, u32[]{:S(2)}) collective-permute-start(bf16[4,320]{1,0:T(4,128)(2,1)S(1)} %get-tuple-element.24), channel_id=1, source_target_pairs={{504,0},{508,4},{0,8},{4,12},{8,16},{12,20},{16,24},{20,28},{24,32... | collective-permute-start | bytes 7688 | tf_op jit(solution)/shard_map/ppermute | solution.py:14
  244.2 6.6 %collective-permute-start.38 = (bf16[4,320]{1,0:T(4,128)(2,1)S(1)}, bf16[4,320]{1,0:T(4,128)(2,1)S(1)}, u32[]{:S(2)}, u32[]{:S(2)}) collective-permute-start(bf16[4,320]{1,0:T(4,128)(2,1)S(1)} %get-tuple-element.23), channel_id=1, source_target_pairs={{500,0},{504,4},{508,8},{0,12},{4,16},{8,20},{12,24},{16,28},{20,3... | collective-permute-start | bytes 7688 | tf_op jit(solution)/shard_map/ppermute | solution.py:14
  250.7 14.3 %collective-permute-start.39 = (bf16[4,320]{1,0:T(4,128)(2,1)S(1)}, bf16[4,320]{1,0:T(4,128)(2,1)S(1)}, u32[]{:S(2)}, u32[]{:S(2)}) collective-permute-start(bf16[4,320]{1,0:T(4,128)(2,1)S(1)} %get-tuple-element.22), channel_id=1, source_target_pairs={{496,0},{500,4},{504,8},{508,12},{0,16},{4,20},{8,24},{12,28},{16,... | collective-permute-start | bytes 7688 | tf_op jit(solution)/shard_map/ppermute | solution.py:14
  265.0 15.6 %collective-permute-start.28 = (f32[4,320]{1,0:T(4,128)S(1)}, f32[4,320]{1,0:T(4,128)S(1)}, u32[]{:S(2)}, u32[]{:S(2)}) collective-permute-start(f32[4,320]{1,0:T(4,128)S(1)} %get-tuple-element.9), channel_id=1, source_target_pairs={{4,0},{8,4},{12,8},{16,12},{20,16},{24,20},{28,24},{32,28},{36,32}... | collective-permute-start | bytes 15368 | tf_op jit(solution)/shard_map/ppermute | solution.py:14
  267.7 35.2 %copy-start.2 = (f32[8,80]{1,0:T(8,128)S(1)}, f32[8,80]{1,0:T(8,128)}, u32[]{:S(2)}) copy-start(f32[8,80]{1,0:T(8,128)} %param.17) | copy-start | bytes 7684
  268.4 12.2 %collective-permute-start.29 = (f32[4,320]{1,0:T(4,128)S(1)}, f32[4,320]{1,0:T(4,128)S(1)}, u32[]{:S(2)}, u32[]{:S(2)}) collective-permute-start(f32[4,320]{1,0:T(4,128)S(1)} %get-tuple-element.8), channel_id=1, source_target_pairs={{8,0},{12,4},{16,8},{20,12},{24,16},{28,20},{32,24},{36,28},{40,32... | collective-permute-start | bytes 15368 | tf_op jit(solution)/shard_map/ppermute | solution.py:14
  271.9 8.8 %collective-permute-start.30 = (f32[4,320]{1,0:T(4,128)S(1)}, f32[4,320]{1,0:T(4,128)S(1)}, u32[]{:S(2)}, u32[]{:S(2)}) collective-permute-start(f32[4,320]{1,0:T(4,128)S(1)} %get-tuple-element.7), channel_id=1, source_target_pairs={{12,0},{16,4},{20,8},{24,12},{28,16},{32,20},{36,24},{40,28},{44,3... | collective-permute-start | bytes 15368 | tf_op jit(solution)/shard_map/ppermute | solution.py:14
  278.7 7.6 %collective-permute-start.31 = (f32[4,320]{1,0:T(4,128)S(1)}, f32[4,320]{1,0:T(4,128)S(1)}, u32[]{:S(2)}, u32[]{:S(2)}) collective-permute-start(f32[4,320]{1,0:T(4,128)S(1)} %get-tuple-element.6), channel_id=1, source_target_pairs={{16,0},{20,4},{24,8},{28,12},{32,16},{36,20},{40,24},{44,28},{48,3... | collective-permute-start | bytes 15368 | tf_op jit(solution)/shard_map/ppermute | solution.py:14
where the time goes:
time: 315 us; the launch traced here: 313 us
  starting transfers between devices  130 us (41%)
  waiting for transfers between devices  83.1 us (26%)
  blocking collectives  71.8 us (23%)
  other arithmetic  13.5 us (4%)
  local copies, waits for them, and re-layouts  8.94 us (3%)
  matrix products  4.21 us (1%)
    ppermute x40, starting transfers between devices, from_behind(): return lax.ppermute(block, axis, route)  130 us
    ppermute x40, waiting for transfers between devices, from_behind(): return lax.ppermute(block, axis, route)  83.1 us
    all_gather x3, blocking collectives, full_rows(): return lax.all_gather(values, 'blk', axis=1, tiled=True)  32.2 us
    psum x2, blocking collectives, local(): summed = lax.psum(partial_value, 'blk')  30.1 us
    psum x1, blocking collectives, local(): indicator = lax.psum(weights, 'blk')  9.47 us
  transfers between devices with their start and end apart: 40, of which 17 were waited for; matrix products, arithmetic and copies ran while one was open for 5% of the time, Pallas kernels for 0%

commit v1 on v0

--- a/solution.py
+++ b/solution.py
@@ -2,6 +2,7 @@
 import jax.numpy as jnp
 from jax import lax
 from jax.sharding import PartitionSpec as P
+from jax.lax import all_to_all, axis_size
 
 MODES = 64
 SWEEPS = 2
@@ -15,7 +16,13 @@
 
 
 def full_rows(values):
-    return lax.all_gather(values, "blk", axis=1, tiled=True)
+    field_press = lambda shard_axis, w_in: jnp.concatenate(
+        all_to_all(
+            jnp.stack([w_in for _ in range(axis_size(shard_axis))], axis=0), shard_axis, 0, 0
+        ),
+        axis=1,
+    )
+    return field_press("blk", values)
 
 
 def local(degree, face_elem, face_side, face_peer, coupling, inv_diag, inv_off, source, residual):

time: 315 us -> 237 us (0.75)
  the two profiles are of different devices: /device:TPU:64 before, /device:TPU:40 now
where the time goes in v1:
time: 237 us; the launch traced here: 236 us
  starting transfers between devices  151 us (64%)
  blocking collectives  39.4 us (17%)
  waiting for transfers between devices  15.4 us (6%)
  other arithmetic  12.9 us (5%)
  local copies, waits for them, and re-layouts  10.9 us (5%)
  matrix products  4.21 us (2%)
    ppermute x40, starting transfers between devices, from_behind(): return lax.ppermute(block, axis, route)  135 us
    psum x2, blocking collectives, local(): summed = lax.psum(partial_value, 'blk')  27.7 us
    all_to_all x3, starting transfers between devices, full_rows(): all_to_all(jnp.stack([w_in for _ in range(axis_size(shard_axis))], axis=0...  16.4 us
    ppermute x40, waiting for transfers between devices, from_behind(): return lax.ppermute(block, axis, route)  15.4 us
    psum x1, blocking collectives, local(): indicator = lax.psum(weights, 'blk')  11.7 us
  transfers between devices with their start and end apart: 43, of which 5 were waited for; matrix products, arithmetic and copies ran while one was open for 6% of the time, Pallas kernels for 0%

profile of v1, /device:TPU:40, one launch (start us, length us, event | category | flops | bytes accessed | tf_op | source)
XLA Modules:
  0.0 235.8 jit_solution(13294777938324677013)
XLA Ops:
  2.9 4.9 %all-to-all-start = ((bf16[4,8,80]{2,1,0:T(8,128)(2,1)}), bf16[4,8,80]{2,1,0:T(8,128)(2,1)S(1)}, u32[]{:S(2)}, u32[]{:S(2)}) async-start(bf16[4,8,80]{2,1,0:T(8,128)(2,1)} %stack.174), calls=%async_computation | async-start | bytes 16384 | tf_op jit(solution)/shard_map/all_to_all | solution.py:20
  12.9 3.8 %collective-permute-start.1 = (s32[4]{0:T(128)S(1)}, s32[4]{0:T(128)S(1)}, u32[]{:S(2)}, u32[]{:S(2)}) collective-permute-start(s32[4]{0:T(128)S(1)} %get-tuple-element.44), channel_id=1, source_target_pairs={{504,0},{508,4},{0,8},{4,12},{8,16},{12,20},{16,24},{20,28},{24,32... | collective-permute-start | bytes 56 | tf_op jit(solution)/shard_map/ppermute | solution.py:15
  16.8 6.4 %collective-permute-start.2 = (s32[4]{0:T(128)S(1)}, s32[4]{0:T(128)S(1)}, u32[]{:S(2)}, u32[]{:S(2)}) collective-permute-start(s32[4]{0:T(128)S(1)} %get-tuple-element.43), channel_id=1, source_target_pairs={{500,0},{504,4},{508,8},{0,12},{4,16},{8,20},{12,24},{16,28},{20,3... | collective-permute-start | bytes 56 | tf_op jit(solution)/shard_map/ppermute | solution.py:15
  23.2 5.2 %collective-permute-start.3 = (s32[4]{0:T(128)S(1)}, s32[4]{0:T(128)S(1)}, u32[]{:S(2)}, u32[]{:S(2)}) collective-permute-start(s32[4]{0:T(128)S(1)} %get-tuple-element.42), channel_id=1, source_target_pairs={{496,0},{500,4},{504,8},{508,12},{0,16},{4,20},{8,24},{12,28},{16,... | collective-permute-start | bytes 56 | tf_op jit(solution)/shard_map/ppermute | solution.py:15
  28.3 1.9 collective-permute-start.4
  32.3 4.9 %collective-permute-start.5 = (s32[4]{0:T(128)S(1)}, s32[4]{0:T(128)S(1)}, u32[]{:S(2)}, u32[]{:S(2)}) collective-permute-start(s32[4]{0:T(128)S(1)} %get-tuple-element.40), channel_id=1, source_target_pairs={{8,0},{12,4},{16,8},{20,12},{24,16},{28,20},{32,24},{36,28},{40,32... | collective-permute-start | bytes 56 | tf_op jit(solution)/shard_map/ppermute | solution.py:15
  37.2 2.4 %collective-permute-start.6 = (s32[4]{0:T(128)S(1)}, s32[4]{0:T(128)S(1)}, u32[]{:S(2)}, u32[]{:S(2)}) collective-permute-start(s32[4]{0:T(128)S(1)} %get-tuple-element.39), channel_id=1, source_target_pairs={{12,0},{16,4},{20,8},{24,12},{28,16},{32,20},{36,24},{40,28},{44,3... | collective-permute-start | bytes 56 | tf_op jit(solution)/shard_map/ppermute | solution.py:15
  39.6 4.8 %collective-permute-start.7 = (s32[4]{0:T(128)S(1)}, s32[4]{0:T(128)S(1)}, u32[]{:S(2)}, u32[]{:S(2)}) collective-permute-start(s32[4]{0:T(128)S(1)} %get-tuple-element.38), channel_id=1, source_target_pairs={{16,0},{20,4},{24,8},{28,12},{32,16},{36,20},{40,24},{44,28},{48,3... | collective-permute-start | bytes 56 | tf_op jit(solution)/shard_map/ppermute | solution.py:15
  49.8 4.8 %all-to-all-start.1 = ((bf16[4,8,80]{2,1,0:T(8,128)(2,1)}), bf16[4,8,80]{2,1,0:T(8,128)(2,1)S(1)}, u32[]{:S(2)}, u32[]{:S(2)}) async-start(bf16[4,8,80]{2,1,0:T(8,128)(2,1)} %stack.193), calls=%async_computation.1 | async-start | bytes 16384 | tf_op jit(solution)/shard_map/all_to_all | solution.py:20
  56.6 1.9 collective-permute-start.8
  58.5 4.5 %collective-permute-start.9 = (f32[4,320]{1,0:T(4,128)S(1)}, f32[4,320]{1,0:T(4,128)S(1)}, u32[]{:S(2)}, u32[]{:S(2)}) collective-permute-start(f32[4,320]{1,0:T(4,128)S(1)} %get-tuple-element.20), channel_id=1, source_target_pairs={{504,0},{508,4},{0,8},{4,12},{8,16},{12,20},{16,24},{20,28},{24,32... | collective-permute-start | bytes 15368 | tf_op jit(solution)/shard_map/ppermute | solution.py:15
  63.0 3.6 %collective-permute-start.10 = (f32[4,320]{1,0:T(4,128)S(1)}, f32[4,320]{1,0:T(4,128)S(1)}, u32[]{:S(2)}, u32[]{:S(2)}) collective-permute-start(f32[4,320]{1,0:T(4,128)S(1)} %get-tuple-element.19), channel_id=1, source_target_pairs={{500,0},{504,4},{508,8},{0,12},{4,16},{8,20},{12,24},{16,28},{20,3... | collective-permute-start | bytes 15368 | tf_op jit(solution)/shard_map/ppermute | solution.py:15
  66.6 5.9 %collective-permute-start.11 = (f32[4,320]{1,0:T(4,128)S(1)}, f32[4,320]{1,0:T(4,128)S(1)}, u32[]{:S(2)}, u32[]{:S(2)}) collective-permute-start(f32[4,320]{1,0:T(4,128)S(1)} %get-tuple-element.18), channel_id=1, source_target_pairs={{496,0},{500,4},{504,8},{508,12},{0,16},{4,20},{8,24},{12,28},{16,... | collective-permute-start | bytes 15368 | tf_op jit(solution)/shard_map/ppermute | solution.py:15
  72.5 1.9 collective-permute-start.12
  75.8 4.3 %collective-permute-start.13 = (f32[4,320]{1,0:T(4,128)S(1)}, f32[4,320]{1,0:T(4,128)S(1)}, u32[]{:S(2)}, u32[]{:S(2)}) collective-permute-start(f32[4,320]{1,0:T(4,128)S(1)} %get-tuple-element.16), channel_id=1, source_target_pairs={{8,0},{12,4},{16,8},{20,12},{24,16},{28,20},{32,24},{36,28},{40,32... | collective-permute-start | bytes 15368 | tf_op jit(solution)/shard_map/ppermute | solution.py:15
  80.2 2.0 collective-permute-start.14
  82.2 3.5 %collective-permute-start.15 = (f32[4,320]{1,0:T(4,128)S(1)}, f32[4,320]{1,0:T(4,128)S(1)}, u32[]{:S(2)}, u32[]{:S(2)}) collective-permute-start(f32[4,320]{1,0:T(4,128)S(1)} %get-tuple-element.14), channel_id=1, source_target_pairs={{16,0},{20,4},{24,8},{28,12},{32,16},{36,20},{40,24},{44,28},{48,3... | collective-permute-start | bytes 15368 | tf_op jit(solution)/shard_map/ppermute | solution.py:15
  85.8 4.7 %collective-permute-start.16 = (bf16[4,320]{1,0:T(4,128)(2,1)S(1)}, bf16[4,320]{1,0:T(4,128)(2,1)S(1)}, u32[]{:S(2)}, u32[]{:S(2)}) collective-permute-start(bf16[4,320]{1,0:T(4,128)(2,1)S(1)} %get-tuple-element.37), channel_id=1, source_target_pairs={{4,0},{8,4},{12,8},{16,12},{20,16},{24,20},{28,24},{32,28},{36,32}... | collective-permute-start | bytes 7688 | tf_op jit(solution)/shard_map/ppermute | solution.py:15
  90.5 3.4 %collective-permute-start.17 = (bf16[4,320]{1,0:T(4,128)(2,1)S(1)}, bf16[4,320]{1,0:T(4,128)(2,1)S(1)}, u32[]{:S(2)}, u32[]{:S(2)}) collective-permute-start(bf16[4,320]{1,0:T(4,128)(2,1)S(1)} %get-tuple-element.36), channel_id=1, source_target_pairs={{8,0},{12,4},{16,8},{20,12},{24,16},{28,20},{32,24},{36,28},{40,32... | collective-permute-start | bytes 7688 | tf_op jit(solution)/shard_map/ppermute | solution.py:15
  93.9 3.3 %collective-permute-start.18 = (bf16[4,320]{1,0:T(4,128)(2,1)S(1)}, bf16[4,320]{1,0:T(4,128)(2,1)S(1)}, u32[]{:S(2)}, u32[]{:S(2)}) collective-permute-start(bf16[4,320]{1,0:T(4,128)(2,1)S(1)} %get-tuple-element.35), channel_id=1, source_target_pairs={{12,0},{16,4},{20,8},{24,12},{28,16},{32,20},{36,24},{40,28},{44,3... | collective-permute-start | bytes 7688 | tf_op jit(solution)/shard_map/ppermute | solution.py:15
  97.3 2.3 collective-permute-start.19
  99.6 2.0 collective-permute-start.20
  102.5 3.6 %collective-permute-start.21 = (bf16[4,320]{1,0:T(4,128)(2,1)S(1)}, bf16[4,320]{1,0:T(4,128)(2,1)S(1)}, u32[]{:S(2)}, u32[]{:S(2)}) collective-permute-start(bf16[4,320]{1,0:T(4,128)(2,1)S(1)} %get-tuple-element.32), channel_id=1, source_target_pairs={{504,0},{508,4},{0,8},{4,12},{8,16},{12,20},{16,24},{20,28},{24,32... | collective-permute-start | bytes 7688 | tf_op jit(solution)/shard_map/ppermute | solution.py:15
  106.2 4.1 %collective-permute-start.22 = (bf16[4,320]{1,0:T(4,128)(2,1)S(1)}, bf16[4,320]{1,0:T(4,128)(2,1)S(1)}, u32[]{:S(2)}, u32[]{:S(2)}) collective-permute-start(bf16[4,320]{1,0:T(4,128)(2,1)S(1)} %get-tuple-element.31), channel_id=1, source_target_pairs={{500,0},{504,4},{508,8},{0,12},{4,16},{8,20},{12,24},{16,28},{20,3... | collective-permute-start | bytes 7688 | tf_op jit(solution)/shard_map/ppermute | solution.py:15
  110.4 2.1 collective-permute-start.23
  112.5 2.8 %collective-permute-done.22 = bf16[4,320]{1,0:T(4,128)(2,1)S(1)} collective-permute-done((bf16[4,320]{1,0:T(4,128)(2,1)S(1)}, bf16[4,320]{1,0:T(4,128)(2,1)S(1)}, u32[]{:S(2)}, u32[]{:S(2)}) %collective-permute-start.22) | collective-permute-done | bytes 2592 | tf_op jit(solution)/shard_map/ppermute | solution.py:15
  115.3 4.7 %collective-permute-done.23 = bf16[4,320]{1,0:T(4,128)(2,1)S(1)} collective-permute-done((bf16[4,320]{1,0:T(4,128)(2,1)S(1)}, bf16[4,320]{1,0:T(4,128)(2,1)S(1)}, u32[]{:S(2)}, u32[]{:S(2)}) %collective-permute-start.23) | collective-permute-done | bytes 2592 | tf_op jit(solution)/shard_map/ppermute | solution.py:15
  122.6 13.8 %psum.21 = bf16[8,320]{1,0:T(8,128)(2,1)S(1)} all-reduce(f32[8,320]{1,0:T(8,128)S(1)} %dynamic_update_slice.6), channel_id=1, replica_groups=mesh['dom'=128,'blk'=4] {'blk'}, use_global_device_ids=true, to_apply=%region_7.8 | all-reduce | flops 2560 | bytes 15360 | tf_op jit(solution)/shard_map/psum | solution.py:105
  139.4 6.7 %all-to-all-start.2 = ((bf16[4,8,80]{2,1,0:T(8,128)(2,1)}), bf16[4,8,80]{2,1,0:T(8,128)(2,1)S(1)}, u32[]{:S(2)}, u32[]{:S(2)}) async-start(bf16[4,8,80]{2,1,0:T(8,128)(2,1)} %stack.221), calls=%async_computation.2 | async-start | bytes 16384 | tf_op jit(solution)/shard_map/all_to_all | solution.py:20
  146.9 1.9 collective-permute-start.24
  148.8 1.9 collective-permute-start.25
  150.7 1.9 collective-permute-start.26
  152.7 1.9 collective-permute-start.27
  154.6 3.6 %collective-permute-start.28 = (f32[4,320]{1,0:T(4,128)S(1)}, f32[4,320]{1,0:T(4,128)S(1)}, u32[]{:S(2)}, u32[]{:S(2)}) collective-permute-start(f32[4,320]{1,0:T(4,128)S(1)} %get-tuple-element.9), channel_id=1, source_target_pairs={{4,0},{8,4},{12,8},{16,12},{20,16},{24,20},{28,24},{32,28},{36,32}... | collective-permute-start | bytes 15368 | tf_op jit(solution)/shard_map/ppermute | solution.py:15
  159.6 7.0 %collective-permute-start.29 = (f32[4,320]{1,0:T(4,128)S(1)}, f32[4,320]{1,0:T(4,128)S(1)}, u32[]{:S(2)}, u32[]{:S(2)}) collective-permute-start(f32[4,320]{1,0:T(4,128)S(1)} %get-tuple-element.8), channel_id=1, source_target_pairs={{8,0},{12,4},{16,8},{20,12},{24,16},{28,20},{32,24},{36,28},{40,32... | collective-permute-start | bytes 15368 | tf_op jit(solution)/shard_map/ppermute | solution.py:15
  166.6 3.2 %collective-permute-start.30 = (f32[4,320]{1,0:T(4,128)S(1)}, f32[4,320]{1,0:T(4,128)S(1)}, u32[]{:S(2)}, u32[]{:S(2)}) collective-permute-start(f32[4,320]{1,0:T(4,128)S(1)} %get-tuple-element.7), channel_id=1, source_target_pairs={{12,0},{16,4},{20,8},{24,12},{28,16},{32,20},{36,24},{40,28},{44,3... | collective-permute-start | bytes 15368 | tf_op jit(solution)/shard_map/ppermute | solution.py:15
  169.9 4.8 %collective-permute-start.31 = (f32[4,320]{1,0:T(4,128)S(1)}, f32[4,320]{1,0:T(4,128)S(1)}, u32[]{:S(2)}, u32[]{:S(2)}) collective-permute-start(f32[4,320]{1,0:T(4,128)S(1)} %get-tuple-element.6), channel_id=1, source_target_pairs={{16,0},{20,4},{24,8},{28,12},{32,16},{36,20},{40,24},{44,28},{48,3... | collective-permute-start | bytes 15368 | tf_op jit(solution)/shard_map/ppermute | solution.py:15
  174.7 3.3 %collective-permute-start.32 = (bf16[4,320]{1,0:T(4,128)(2,1)S(1)}, bf16[4,320]{1,0:T(4,128)(2,1)S(1)}, u32[]{:S(2)}, u32[]{:S(2)}) collective-permute-start(bf16[4,320]{1,0:T(4,128)(2,1)S(1)} %get-tuple-element.29), channel_id=1, source_target_pairs={{4,0},{8,4},{12,8},{16,12},{20,16},{24,20},{28,24},{32,28},{36,32}... | collective-permute-start | bytes 7688 | tf_op jit(solution)/shard_map/ppermute | solution.py:15
  178.0 2.5 %collective-permute-start.33 = (bf16[4,320]{1,0:T(4,128)(2,1)S(1)}, bf16[4,320]{1,0:T(4,128)(2,1)S(1)}, u32[]{:S(2)}, u32[]{:S(2)}) collective-permute-start(bf16[4,320]{1,0:T(4,128)(2,1)S(1)} %get-tuple-element.28), channel_id=1, source_target_pairs={{8,0},{12,4},{16,8},{20,12},{24,16},{28,20},{32,24},{36,28},{40,32... | collective-permute-start | bytes 7688 | tf_op jit(solution)/shard_map/ppermute | solution.py:15
  180.5 1.9 collective-permute-start.34
  182.5 2.2 collective-permute-start.35
  184.7 2.0 collective-permute-start.36
  187.7 3.6 %collective-permute-start.37 = (bf16[4,320]{1,0:T(4,128)(2,1)S(1)}, bf16[4,320]{1,0:T(4,128)(2,1)S(1)}, u32[]{:S(2)}, u32[]{:S(2)}) collective-permute-start(bf16[4,320]{1,0:T(4,128)(2,1)S(1)} %get-tuple-element.24), channel_id=1, source_target_pairs={{504,0},{508,4},{0,8},{4,12},{8,16},{12,20},{16,24},{20,28},{24,32... | collective-permute-start | bytes 7688 | tf_op jit(solution)/shard_map/ppermute | solution.py:15
  191.3 5.4 %collective-permute-start.38 = (bf16[4,320]{1,0:T(4,128)(2,1)S(1)}, bf16[4,320]{1,0:T(4,128)(2,1)S(1)}, u32[]{:S(2)}, u32[]{:S(2)}) collective-permute-start(bf16[4,320]{1,0:T(4,128)(2,1)S(1)} %get-tuple-element.23), channel_id=1, source_target_pairs={{500,0},{504,4},{508,8},{0,12},{4,16},{8,20},{12,24},{16,28},{20,3... | collective-permute-start | bytes 7688 | tf_op jit(solution)/shard_map/ppermute | solution.py:15
  196.7 3.3 %collective-permute-start.39 = (bf16[4,320]{1,0:T(4,128)(2,1)S(1)}, bf16[4,320]{1,0:T(4,128)(2,1)S(1)}, u32[]{:S(2)}, u32[]{:S(2)}) collective-permute-start(bf16[4,320]{1,0:T(4,128)(2,1)S(1)} %get-tuple-element.22), channel_id=1, source_target_pairs={{496,0},{500,4},{504,8},{508,12},{0,16},{4,20},{8,24},{12,28},{16,... | collective-permute-start | bytes 7688 | tf_op jit(solution)/shard_map/ppermute | solution.py:15
  200.5 6.0 %collective-permute-done.39 = bf16[4,320]{1,0:T(4,128)(2,1)S(1)} collective-permute-done((bf16[4,320]{1,0:T(4,128)(2,1)S(1)}, bf16[4,320]{1,0:T(4,128)(2,1)S(1)}, u32[]{:S(2)}, u32[]{:S(2)}) %collective-permute-start.39) | collective-permute-done | bytes 2592 | tf_op jit(solution)/shard_map/ppermute | solution.py:15
  209.0 13.8 %psum.22 = bf16[8,320]{1,0:T(8,128)(2,1)S(1)} all-reduce(f32[8,320]{1,0:T(8,128)S(1)} %dynamic_update_slice.7), channel_id=1, replica_groups=mesh['dom'=128,'blk'=4] {'blk'}, use_global_device_ids=true, to_apply=%region_12.13 | all-reduce | flops 2560 | bytes 15360 | tf_op jit(solution)/shard_map/psum | solution.py:105
  224.1 11.7 %psum.23 = f32[8]{0:T(128)} all-reduce(f32[8]{0:T(128)S(1)} %get-tuple-element.2), channel_id=1, replica_groups=mesh['dom'=128,'blk'=4] {'blk'}, use_global_device_ids=true, to_apply=%region_14.15 | all-reduce | flops 8 | bytes 64 | tf_op jit(solution)/shard_map/psum | solution.py:109
  (166 shorter events, 31.8 us)
Async XLA Ops:
  0.6 53.9 %copy-start = (bf16[32,80,320]{2,1,0:T(8,128)(2,1)S(1)}, bf16[32,80,320]{2,1,0:T(8,128)(2,1)}, u32[]{:S(2)}) copy-start(bf16[32,80,320]{2,1,0:T(8,128)(2,1)} %param.13) | copy-start | bytes 4915204
  2.9 43.4 %all-to-all-start = ((bf16[4,8,80]{2,1,0:T(8,128)(2,1)}), bf16[4,8,80]{2,1,0:T(8,128)(2,1)S(1)}, u32[]{:S(2)}, u32[]{:S(2)}) async-start(bf16[4,8,80]{2,1,0:T(8,128)(2,1)} %stack.174), calls=%async_computation | async-start | bytes 16384 | tf_op jit(solution)/shard_map/all_to_all | solution.py:20
  11.0 21.3 %collective-permute-start = (s32[4]{0:T(128)S(1)}, s32[4]{0:T(128)S(1)}, u32[]{:S(2)}, u32[]{:S(2)}) collective-permute-start(s32[4]{0:T(128)S(1)} %get-tuple-element.45), channel_id=1, source_target_pairs={{508,0},{0,4},{4,8},{8,12},{12,16},{16,20},{20,24},{24,28},{28,32}... | collective-permute-start | bytes 56 | tf_op jit(solution)/shard_map/ppermute | solution.py:15
  12.9 24.3 %collective-permute-start.1 = (s32[4]{0:T(128)S(1)}, s32[4]{0:T(128)S(1)}, u32[]{:S(2)}, u32[]{:S(2)}) collective-permute-start(s32[4]{0:T(128)S(1)} %get-tuple-element.44), channel_id=1, source_target_pairs={{504,0},{508,4},{0,8},{4,12},{8,16},{12,20},{16,24},{20,28},{24,32... | collective-permute-start | bytes 56 | tf_op jit(solution)/shard_map/ppermute | solution.py:15
  16.8 22.8 %collective-permute-start.2 = (s32[4]{0:T(128)S(1)}, s32[4]{0:T(128)S(1)}, u32[]{:S(2)}, u32[]{:S(2)}) collective-permute-start(s32[4]{0:T(128)S(1)} %get-tuple-element.43), channel_id=1, source_target_pairs={{500,0},{504,4},{508,8},{0,12},{4,16},{8,20},{12,24},{16,28},{20,3... | collective-permute-start | bytes 56 | tf_op jit(solution)/shard_map/ppermute | solution.py:15
  23.2 21.3 %collective-permute-start.3 = (s32[4]{0:T(128)S(1)}, s32[4]{0:T(128)S(1)}, u32[]{:S(2)}, u32[]{:S(2)}) collective-permute-start(s32[4]{0:T(128)S(1)} %get-tuple-element.42), channel_id=1, source_target_pairs={{496,0},{500,4},{504,8},{508,12},{0,16},{4,20},{8,24},{12,28},{16,... | collective-permute-start | bytes 56 | tf_op jit(solution)/shard_map/ppermute | solution.py:15
  28.3 16.1 %collective-permute-start.4 = (s32[4]{0:T(128)S(1)}, s32[4]{0:T(128)S(1)}, u32[]{:S(2)}, u32[]{:S(2)}) collective-permute-start(s32[4]{0:T(128)S(1)} %get-tuple-element.41), channel_id=1, source_target_pairs={{4,0},{8,4},{12,8},{16,12},{20,16},{24,20},{28,24},{32,28},{36,32}... | collective-permute-start | bytes 56 | tf_op jit(solution)/shard_map/ppermute | solution.py:15
  32.3 12.2 %collective-permute-start.5 = (s32[4]{0:T(128)S(1)}, s32[4]{0:T(128)S(1)}, u32[]{:S(2)}, u32[]{:S(2)}) collective-permute-start(s32[4]{0:T(128)S(1)} %get-tuple-element.40), channel_id=1, source_target_pairs={{8,0},{12,4},{16,8},{20,12},{24,16},{28,20},{32,24},{36,28},{40,32... | collective-permute-start | bytes 56 | tf_op jit(solution)/shard_map/ppermute | solution.py:15
  37.2 7.3 %collective-permute-start.6 = (s32[4]{0:T(128)S(1)}, s32[4]{0:T(128)S(1)}, u32[]{:S(2)}, u32[]{:S(2)}) collective-permute-start(s32[4]{0:T(128)S(1)} %get-tuple-element.39), channel_id=1, source_target_pairs={{12,0},{16,4},{20,8},{24,12},{28,16},{32,20},{36,24},{40,28},{44,3... | collective-permute-start | bytes 56 | tf_op jit(solution)/shard_map/ppermute | solution.py:15
  39.6 6.4 %collective-permute-start.7 = (s32[4]{0:T(128)S(1)}, s32[4]{0:T(128)S(1)}, u32[]{:S(2)}, u32[]{:S(2)}) collective-permute-start(s32[4]{0:T(128)S(1)} %get-tuple-element.38), channel_id=1, source_target_pairs={{16,0},{20,4},{24,8},{28,12},{32,16},{36,20},{40,24},{44,28},{48,3... | collective-permute-start | bytes 56 | tf_op jit(solution)/shard_map/ppermute | solution.py:15
  49.8 24.7 %all-to-all-start.1 = ((bf16[4,8,80]{2,1,0:T(8,128)(2,1)}), bf16[4,8,80]{2,1,0:T(8,128)(2,1)S(1)}, u32[]{:S(2)}, u32[]{:S(2)}) async-start(bf16[4,8,80]{2,1,0:T(8,128)(2,1)} %stack.193), calls=%async_computation.1 | async-start | bytes 16384 | tf_op jit(solution)/shard_map/all_to_all | solution.py:20
  56.6 19.2 %collective-permute-start.8 = (f32[4,320]{1,0:T(4,128)S(1)}, f32[4,320]{1,0:T(4,128)S(1)}, u32[]{:S(2)}, u32[]{:S(2)}) collective-permute-start(f32[4,320]{1,0:T(4,128)S(1)} %get-tuple-element.21), channel_id=1, source_target_pairs={{508,0},{0,4},{4,8},{8,12},{12,16},{16,20},{20,24},{24,28},{28,32}... | collective-permute-start | bytes 15368 | tf_op jit(solution)/shard_map/ppermute | solution.py:15
  58.5 21.7 %collective-permute-start.9 = (f32[4,320]{1,0:T(4,128)S(1)}, f32[4,320]{1,0:T(4,128)S(1)}, u32[]{:S(2)}, u32[]{:S(2)}) collective-permute-start(f32[4,320]{1,0:T(4,128)S(1)} %get-tuple-element.20), channel_id=1, source_target_pairs={{504,0},{508,4},{0,8},{4,12},{8,16},{12,20},{16,24},{20,28},{24,32... | collective-permute-start | bytes 15368 | tf_op jit(solution)/shard_map/ppermute | solution.py:15
  63.0 19.2 %collective-permute-start.10 = (f32[4,320]{1,0:T(4,128)S(1)}, f32[4,320]{1,0:T(4,128)S(1)}, u32[]{:S(2)}, u32[]{:S(2)}) collective-permute-start(f32[4,320]{1,0:T(4,128)S(1)} %get-tuple-element.19), channel_id=1, source_target_pairs={{500,0},{504,4},{508,8},{0,12},{4,16},{8,20},{12,24},{16,28},{20,3... | collective-permute-start | bytes 15368 | tf_op jit(solution)/shard_map/ppermute | solution.py:15
  66.6 19.1 %collective-permute-start.11 = (f32[4,320]{1,0:T(4,128)S(1)}, f32[4,320]{1,0:T(4,128)S(1)}, u32[]{:S(2)}, u32[]{:S(2)}) collective-permute-start(f32[4,320]{1,0:T(4,128)S(1)} %get-tuple-element.18), channel_id=1, source_target_pairs={{496,0},{500,4},{504,8},{508,12},{0,16},{4,20},{8,24},{12,28},{16,... | collective-permute-start | bytes 15368 | tf_op jit(solution)/shard_map/ppermute | solution.py:15
  72.5 18.1 %collective-permute-start.12 = (f32[4,320]{1,0:T(4,128)S(1)}, f32[4,320]{1,0:T(4,128)S(1)}, u32[]{:S(2)}, u32[]{:S(2)}) collective-permute-start(f32[4,320]{1,0:T(4,128)S(1)} %get-tuple-element.17), channel_id=1, source_target_pairs={{4,0},{8,4},{12,8},{16,12},{20,16},{24,20},{28,24},{32,28},{36,32}... | collective-permute-start | bytes 15368 | tf_op jit(solution)/shard_map/ppermute | solution.py:15
  75.8 60.8 %copy-start.3 = (bf16[8,80,320]{2,1,0:T(8,128)(2,1)S(1)}, bf16[8,80,320]{2,1,0:T(8,128)(2,1)}, u32[]{:S(2)}) copy-start(bf16[8,80,320]{2,1,0:T(8,128)(2,1)} %param.15) | copy-start | bytes 1228804
  75.8 18.1 %collective-permute-start.13 = (f32[4,320]{1,0:T(4,128)S(1)}, f32[4,320]{1,0:T(4,128)S(1)}, u32[]{:S(2)}, u32[]{:S(2)}) collective-permute-start(f32[4,320]{1,0:T(4,128)S(1)} %get-tuple-element.16), channel_id=1, source_target_pairs={{8,0},{12,4},{16,8},{20,12},{24,16},{28,20},{32,24},{36,28},{40,32... | collective-permute-start | bytes 15368 | tf_op jit(solution)/shard_map/ppermute | solution.py:15
  80.2 17.1 %collective-permute-start.14 = (f32[4,320]{1,0:T(4,128)S(1)}, f32[4,320]{1,0:T(4,128)S(1)}, u32[]{:S(2)}, u32[]{:S(2)}) collective-permute-start(f32[4,320]{1,0:T(4,128)S(1)} %get-tuple-element.15), channel_id=1, source_target_pairs={{12,0},{16,4},{20,8},{24,12},{28,16},{32,20},{36,24},{40,28},{44,3... | collective-permute-start | bytes 15368 | tf_op jit(solution)/shard_map/ppermute | solution.py:15
  82.2 17.3 %collective-permute-start.15 = (f32[4,320]{1,0:T(4,128)S(1)}, f32[4,320]{1,0:T(4,128)S(1)}, u32[]{:S(2)}, u32[]{:S(2)}) collective-permute-start(f32[4,320]{1,0:T(4,128)S(1)} %get-tuple-element.14), channel_id=1, source_target_pairs={{16,0},{20,4},{24,8},{28,12},{32,16},{36,20},{40,24},{44,28},{48,3... | collective-permute-start | bytes 15368 | tf_op jit(solution)/shard_map/ppermute | solution.py:15
  85.8 16.8 %collective-permute-start.16 = (bf16[4,320]{1,0:T(4,128)(2,1)S(1)}, bf16[4,320]{1,0:T(4,128)(2,1)S(1)}, u32[]{:S(2)}, u32[]{:S(2)}) collective-permute-start(bf16[4,320]{1,0:T(4,128)(2,1)S(1)} %get-tuple-element.37), channel_id=1, source_target_pairs={{4,0},{8,4},{12,8},{16,12},{20,16},{24,20},{28,24},{32,28},{36,32}... | collective-permute-start | bytes 7688 | tf_op jit(solution)/shard_map/ppermute | solution.py:15
  90.5 15.6 %collective-permute-start.17 = (bf16[4,320]{1,0:T(4,128)(2,1)S(1)}, bf16[4,320]{1,0:T(4,128)(2,1)S(1)}, u32[]{:S(2)}, u32[]{:S(2)}) collective-permute-start(bf16[4,320]{1,0:T(4,128)(2,1)S(1)} %get-tuple-element.36), channel_id=1, source_target_pairs={{8,0},{12,4},{16,8},{20,12},{24,16},{28,20},{32,24},{36,28},{40,32... | collective-permute-start | bytes 7688 | tf_op jit(solution)/shard_map/ppermute | solution.py:15
  93.9 16.4 %collective-permute-start.18 = (bf16[4,320]{1,0:T(4,128)(2,1)S(1)}, bf16[4,320]{1,0:T(4,128)(2,1)S(1)}, u32[]{:S(2)}, u32[]{:S(2)}) collective-permute-start(bf16[4,320]{1,0:T(4,128)(2,1)S(1)} %get-tuple-element.35), channel_id=1, source_target_pairs={{12,0},{16,4},{20,8},{24,12},{28,16},{32,20},{36,24},{40,28},{44,3... | collective-permute-start | bytes 7688 | tf_op jit(solution)/shard_map/ppermute | solution.py:15
  97.3 15.2 %collective-permute-start.19 = (bf16[4,320]{1,0:T(4,128)(2,1)S(1)}, bf16[4,320]{1,0:T(4,128)(2,1)S(1)}, u32[]{:S(2)}, u32[]{:S(2)}) collective-permute-start(bf16[4,320]{1,0:T(4,128)(2,1)S(1)} %get-tuple-element.34), channel_id=1, source_target_pairs={{16,0},{20,4},{24,8},{28,12},{32,16},{36,20},{40,24},{44,28},{48,3... | collective-permute-start | bytes 7688 | tf_op jit(solution)/shard_map/ppermute | solution.py:15
  99.6 12.9 %collective-permute-start.20 = (bf16[4,320]{1,0:T(4,128)(2,1)S(1)}, bf16[4,320]{1,0:T(4,128)(2,1)S(1)}, u32[]{:S(2)}, u32[]{:S(2)}) collective-permute-start(bf16[4,320]{1,0:T(4,128)(2,1)S(1)} %get-tuple-element.33), channel_id=1, source_target_pairs={{508,0},{0,4},{4,8},{8,12},{12,16},{16,20},{20,24},{24,28},{28,32}... | collective-permute-start | bytes 7688 | tf_op jit(solution)/shard_map/ppermute | solution.py:15
  101.6 35.2 %copy-start.1 = (f32[8,80]{1,0:T(8,128)S(1)}, f32[8,80]{1,0:T(8,128)}, u32[]{:S(2)}) copy-start(f32[8,80]{1,0:T(8,128)} %param.14) | copy-start | bytes 7684
  102.5 10.0 %collective-permute-start.21 = (bf16[4,320]{1,0:T(4,128)(2,1)S(1)}, bf16[4,320]{1,0:T(4,128)(2,1)S(1)}, u32[]{:S(2)}, u32[]{:S(2)}) collective-permute-start(bf16[4,320]{1,0:T(4,128)(2,1)S(1)} %get-tuple-element.32), channel_id=1, source_target_pairs={{504,0},{508,4},{0,8},{4,12},{8,16},{12,20},{16,24},{20,28},{24,32... | collective-permute-start | bytes 7688 | tf_op jit(solution)/shard_map/ppermute | solution.py:15
  106.2 9.1 %collective-permute-start.22 = (bf16[4,320]{1,0:T(4,128)(2,1)S(1)}, bf16[4,320]{1,0:T(4,128)(2,1)S(1)}, u32[]{:S(2)}, u32[]{:S(2)}) collective-permute-start(bf16[4,320]{1,0:T(4,128)(2,1)S(1)} %get-tuple-element.31), channel_id=1, source_target_pairs={{500,0},{504,4},{508,8},{0,12},{4,16},{8,20},{12,24},{16,28},{20,3... | collective-permute-start | bytes 7688 | tf_op jit(solution)/shard_map/ppermute | solution.py:15
  110.4 9.7 %collective-permute-start.23 = (bf16[4,320]{1,0:T(4,128)(2,1)S(1)}, bf16[4,320]{1,0:T(4,128)(2,1)S(1)}, u32[]{:S(2)}, u32[]{:S(2)}) collective-permute-start(bf16[4,320]{1,0:T(4,128)(2,1)S(1)} %get-tuple-element.30), channel_id=1, source_target_pairs={{496,0},{500,4},{504,8},{508,12},{0,16},{4,20},{8,24},{12,28},{16,... | collective-permute-start | bytes 7688 | tf_op jit(solution)/shard_map/ppermute | solution.py:15
  139.4 18.9 %all-to-all-start.2 = ((bf16[4,8,80]{2,1,0:T(8,128)(2,1)}), bf16[4,8,80]{2,1,0:T(8,128)(2,1)S(1)}, u32[]{:S(2)}, u32[]{:S(2)}) async-start(bf16[4,8,80]{2,1,0:T(8,128)(2,1)} %stack.221), calls=%async_computation.2 | async-start | bytes 16384 | tf_op jit(solution)/shard_map/all_to_all | solution.py:20
  146.9 12.8 %collective-permute-start.24 = (f32[4,320]{1,0:T(4,128)S(1)}, f32[4,320]{1,0:T(4,128)S(1)}, u32[]{:S(2)}, u32[]{:S(2)}) collective-permute-start(f32[4,320]{1,0:T(4,128)S(1)} %get-tuple-element.13), channel_id=1, source_target_pairs={{508,0},{0,4},{4,8},{8,12},{12,16},{16,20},{20,24},{24,28},{28,32}... | collective-permute-start | bytes 15368 | tf_op jit(solution)/shard_map/ppermute | solution.py:15
  148.8 17.8 %collective-permute-start.25 = (f32[4,320]{1,0:T(4,128)S(1)}, f32[4,320]{1,0:T(4,128)S(1)}, u32[]{:S(2)}, u32[]{:S(2)}) collective-permute-start(f32[4,320]{1,0:T(4,128)S(1)} %get-tuple-element.12), channel_id=1, source_target_pairs={{504,0},{508,4},{0,8},{4,12},{8,16},{12,20},{16,24},{20,28},{24,32... | collective-permute-start | bytes 15368 | tf_op jit(solution)/shard_map/ppermute | solution.py:15
  150.7 19.1 %collective-permute-start.26 = (f32[4,320]{1,0:T(4,128)S(1)}, f32[4,320]{1,0:T(4,128)S(1)}, u32[]{:S(2)}, u32[]{:S(2)}) collective-permute-start(f32[4,320]{1,0:T(4,128)S(1)} %get-tuple-element.11), channel_id=1, source_target_pairs={{500,0},{504,4},{508,8},{0,12},{4,16},{8,20},{12,24},{16,28},{20,3... | collective-permute-start | bytes 15368 | tf_op jit(solution)/shard_map/ppermute | solution.py:15
  152.7 22.0 %collective-permute-start.27 = (f32[4,320]{1,0:T(4,128)S(1)}, f32[4,320]{1,0:T(4,128)S(1)}, u32[]{:S(2)}, u32[]{:S(2)}) collective-permute-start(f32[4,320]{1,0:T(4,128)S(1)} %get-tuple-element.10), channel_id=1, source_target_pairs={{496,0},{500,4},{504,8},{508,12},{0,16},{4,20},{8,24},{12,28},{16,... | collective-permute-start | bytes 15368 | tf_op jit(solution)/shard_map/ppermute | solution.py:15
  154.6 23.4 %collective-permute-start.28 = (f32[4,320]{1,0:T(4,128)S(1)}, f32[4,320]{1,0:T(4,128)S(1)}, u32[]{:S(2)}, u32[]{:S(2)}) collective-permute-start(f32[4,320]{1,0:T(4,128)S(1)} %get-tuple-element.9), channel_id=1, source_target_pairs={{4,0},{8,4},{12,8},{16,12},{20,16},{24,20},{28,24},{32,28},{36,32}... | collective-permute-start | bytes 15368 | tf_op jit(solution)/shard_map/ppermute | solution.py:15
  159.6 20.9 %collective-permute-start.29 = (f32[4,320]{1,0:T(4,128)S(1)}, f32[4,320]{1,0:T(4,128)S(1)}, u32[]{:S(2)}, u32[]{:S(2)}) collective-permute-start(f32[4,320]{1,0:T(4,128)S(1)} %get-tuple-element.8), channel_id=1, source_target_pairs={{8,0},{12,4},{16,8},{20,12},{24,16},{28,20},{32,24},{36,28},{40,32... | collective-permute-start | bytes 15368 | tf_op jit(solution)/shard_map/ppermute | solution.py:15
  166.6 15.8 %collective-permute-start.30 = (f32[4,320]{1,0:T(4,128)S(1)}, f32[4,320]{1,0:T(4,128)S(1)}, u32[]{:S(2)}, u32[]{:S(2)}) collective-permute-start(f32[4,320]{1,0:T(4,128)S(1)} %get-tuple-element.7), channel_id=1, source_target_pairs={{12,0},{16,4},{20,8},{24,12},{28,16},{32,20},{36,24},{40,28},{44,3... | collective-permute-start | bytes 15368 | tf_op jit(solution)/shard_map/ppermute | solution.py:15
  169.9 14.8 %collective-permute-start.31 = (f32[4,320]{1,0:T(4,128)S(1)}, f32[4,320]{1,0:T(4,128)S(1)}, u32[]{:S(2)}, u32[]{:S(2)}) collective-permute-start(f32[4,320]{1,0:T(4,128)S(1)} %get-tuple-element.6), channel_id=1, source_target_pairs={{16,0},{20,4},{24,8},{28,12},{32,16},{36,20},{40,24},{44,28},{48,3... | collective-permute-start | bytes 15368 | tf_op jit(solution)/shard_map/ppermute | solution.py:15
  174.7 12.9 %collective-permute-start.32 = (bf16[4,320]{1,0:T(4,128)(2,1)S(1)}, bf16[4,320]{1,0:T(4,128)(2,1)S(1)}, u32[]{:S(2)}, u32[]{:S(2)}) collective-permute-start(bf16[4,320]{1,0:T(4,128)(2,1)S(1)} %get-tuple-element.29), channel_id=1, source_target_pairs={{4,0},{8,4},{12,8},{16,12},{20,16},{24,20},{28,24},{32,28},{36,32}... | collective-permute-start | bytes 7688 | tf_op jit(solution)/shard_map/ppermute | solution.py:15
  178.0 13.3 %collective-permute-start.33 = (bf16[4,320]{1,0:T(4,128)(2,1)S(1)}, bf16[4,320]{1,0:T(4,128)(2,1)S(1)}, u32[]{:S(2)}, u32[]{:S(2)}) collective-permute-start(bf16[4,320]{1,0:T(4,128)(2,1)S(1)} %get-tuple-element.28), channel_id=1, source_target_pairs={{8,0},{12,4},{16,8},{20,12},{24,16},{28,20},{32,24},{36,28},{40,32... | collective-permute-start | bytes 7688 | tf_op jit(solution)/shard_map/ppermute | solution.py:15
  180.5 16.2 %collective-permute-start.34 = (bf16[4,320]{1,0:T(4,128)(2,1)S(1)}, bf16[4,320]{1,0:T(4,128)(2,1)S(1)}, u32[]{:S(2)}, u32[]{:S(2)}) collective-permute-start(bf16[4,320]{1,0:T(4,128)(2,1)S(1)} %get-tuple-element.27), channel_id=1, source_target_pairs={{12,0},{16,4},{20,8},{24,12},{28,16},{32,20},{36,24},{40,28},{44,3... | collective-permute-start | bytes 7688 | tf_op jit(solution)/shard_map/ppermute | solution.py:15
  182.5 17.6 %collective-permute-start.35 = (bf16[4,320]{1,0:T(4,128)(2,1)S(1)}, bf16[4,320]{1,0:T(4,128)(2,1)S(1)}, u32[]{:S(2)}, u32[]{:S(2)}) collective-permute-start(bf16[4,320]{1,0:T(4,128)(2,1)S(1)} %get-tuple-element.26), channel_id=1, source_target_pairs={{16,0},{20,4},{24,8},{28,12},{32,16},{36,20},{40,24},{44,28},{48,3... | collective-permute-start | bytes 7688 | tf_op jit(solution)/shard_map/ppermute | solution.py:15
  184.7 15.4 %collective-permute-start.36 = (bf16[4,320]{1,0:T(4,128)(2,1)S(1)}, bf16[4,320]{1,0:T(4,128)(2,1)S(1)}, u32[]{:S(2)}, u32[]{:S(2)}) collective-permute-start(bf16[4,320]{1,0:T(4,128)(2,1)S(1)} %get-tuple-element.25), channel_id=1, source_target_pairs={{508,0},{0,4},{4,8},{8,12},{12,16},{16,20},{20,24},{24,28},{28,32}... | collective-permute-start | bytes 7688 | tf_op jit(solution)/shard_map/ppermute | solution.py:15
  186.8 36.5 %copy-start.2 = (f32[8,80]{1,0:T(8,128)S(1)}, f32[8,80]{1,0:T(8,128)}, u32[]{:S(2)}) copy-start(f32[8,80]{1,0:T(8,128)} %param.17) | copy-start | bytes 7684
  187.7 12.4 %collective-permute-start.37 = (bf16[4,320]{1,0:T(4,128)(2,1)S(1)}, bf16[4,320]{1,0:T(4,128)(2,1)S(1)}, u32[]{:S(2)}, u32[]{:S(2)}) collective-permute-start(bf16[4,320]{1,0:T(4,128)(2,1)S(1)} %get-tuple-element.24), channel_id=1, source_target_pairs={{504,0},{508,4},{0,8},{4,12},{8,16},{12,20},{16,24},{20,28},{24,32... | collective-permute-start | bytes 7688 | tf_op jit(solution)/shard_map/ppermute | solution.py:15
  191.3 9.1 %collective-permute-start.38 = (bf16[4,320]{1,0:T(4,128)(2,1)S(1)}, bf16[4,320]{1,0:T(4,128)(2,1)S(1)}, u32[]{:S(2)}, u32[]{:S(2)}) collective-permute-start(bf16[4,320]{1,0:T(4,128)(2,1)S(1)} %get-tuple-element.23), channel_id=1, source_target_pairs={{500,0},{504,4},{508,8},{0,12},{4,16},{8,20},{12,24},{16,28},{20,3... | collective-permute-start | bytes 7688 | tf_op jit(solution)/shard_map/ppermute | solution.py:15
  196.7 9.7 %collective-permute-start.39 = (bf16[4,320]{1,0:T(4,128)(2,1)S(1)}, bf16[4,320]{1,0:T(4,128)(2,1)S(1)}, u32[]{:S(2)}, u32[]{:S(2)}) collective-permute-start(bf16[4,320]{1,0:T(4,128)(2,1)S(1)} %get-tuple-element.22), channel_id=1, source_target_pairs={{496,0},{500,4},{504,8},{508,12},{0,16},{4,20},{8,24},{12,28},{16,... | collective-permute-start | bytes 7688 | tf_op jit(solution)/shard_map/ppermute | solution.py:15
